TPU v7x, 32 devices: a whole 2x2x4 slice. The times are simulated.
32 devices in a mesh: grid: 8 (over z, x), chan: 4 (over y, core).
Axes of the slice: x: 2, y: 2, z: 4, core: 2. Of those that a mesh axis runs over, the one named last changes fastest.
Arguments:
- input_field: bfloat16 [256, 1024, 1024], P('chan', 'grid'), may hold values from -6 to 6
- out_cotangent: bfloat16 [256, 1024, 1024], P('chan', 'grid'), may hold values from -6 to 6
- core_first: float32 [256, 16], replicated, may hold values from -1.5 to 1.5
- core_second: float32 [16, 256, 16], replicated, may hold values from -1.5 to 1.5
- core_third: float32 [16, 128, 16], replicated, may hold values from -1.5 to 1.5
- column_mode_core: float32 [2, 16, 128], replicated, may hold values from -2 to 2
Outputs:
- output_field: bfloat16 [256, 1024, 1024], P('chan', 'grid')
- input_grad: bfloat16 [256, 1024, 1024], P('chan', 'grid')
- grad_first: float32 [256, 16], replicated
- grad_second: float32 [16, 256, 16], replicated
- grad_third: float32 [16, 128, 16], replicated
- grad_fourth: float32 [2, 16, 128], replicated
All inputs are finite; a program needn't handle non-finite values.
Results may differ from a plain program's by a relative error of at most 0.0079.
Values may be sent and summed in bfloat16 or wider, within the bound.
A program may use at most 128 MiB of HBM per device.

v0:
```python
import math

import jax
import jax.numpy as jnp
from jax import lax
from jax.sharding import PartitionSpec as P

GRID_SIDE = 1024
MODES_X = 128
MODES_Y = 128


full_turn = 2.0 * math.pi


def turn_tables(mode_index, row_index):
    freq = jnp.where(mode_index < MODES_X // 2, mode_index, GRID_SIDE - MODES_X + mode_index)
    phase = freq[:, None] * row_index[None, :] % GRID_SIDE
    angle = phase.astype(jnp.float32) * (full_turn / GRID_SIDE)
    cosine = jnp.cos(angle).astype(jnp.bfloat16)
    sine = jnp.sin(angle).astype(jnp.bfloat16)
    real_rows = jnp.stack([cosine, sine], axis=-1)
    imag_rows = jnp.stack([-sine, cosine], axis=-1)
    return jnp.stack([real_rows, imag_rows], axis=1)


def width_table():
    column = jnp.arange(GRID_SIDE, dtype=jnp.int32)
    wave = jnp.arange(MODES_Y, dtype=jnp.int32)
    phase = column[:, None] * wave[None, :] % GRID_SIDE
    angle = phase.astype(jnp.float32) * (full_turn / GRID_SIDE)
    cosine = jnp.cos(angle).astype(jnp.bfloat16)
    sine = jnp.sin(angle).astype(jnp.bfloat16)
    return jnp.stack([cosine, -sine], axis=1)


def local(input_field, out_cotangent, core_first, core_second, core_third, column_mode_core):
    highest_accuracy = lax.Precision.HIGHEST
    grid_count = lax.axis_size("grid")
    grid_index = lax.axis_index("grid")
    chan_index = lax.axis_index("chan")
    chan_dev = input_field.shape[0]
    rows_dev = input_field.shape[1]
    modes_dev = MODES_X // grid_count
    base = width_table()
    forward_table = base.reshape(GRID_SIDE, 2 * MODES_Y)

    def column_modes(field):
        product = jnp.dot(
            field.reshape(chan_dev * rows_dev, GRID_SIDE),
            forward_table,
            preferred_element_type=jnp.float32,
        )
        return product.astype(jnp.bfloat16).reshape(chan_dev, rows_dev, 2, MODES_Y)

    both_rows = jnp.stack([column_modes(input_field), column_modes(out_cotangent)])
    mode_index = jnp.arange(MODES_X, dtype=jnp.int32)
    own_rows = grid_index * rows_dev + jnp.arange(rows_dev, dtype=jnp.int32)
    own_tables = turn_tables(mode_index, own_rows)
    tables = own_tables
    spectra = lax.psum_scatter(
        jnp.einsum("kphq,fchqy->kfcpy", tables, both_rows, preferred_element_type=jnp.float32),
        "grid",
        scatter_dimension=0,
        tiled=True,
    )
    weight_c = jnp.where(jnp.arange(MODES_Y, dtype=jnp.int32) == 0, 1.0, 2.0).astype(jnp.float32)
    spec_in = spectra[:, 0] * (1.0 / GRID_SIDE)
    spec_grad = spectra[:, 1] * (weight_c / GRID_SIDE)
    first_local = lax.dynamic_slice_in_dim(core_first, chan_index * chan_dev, chan_dev, 0)
    second_local = lax.dynamic_slice_in_dim(core_second, chan_index * chan_dev, chan_dev, 1)
    third_core_local = lax.dynamic_slice_in_dim(core_third, grid_index * modes_dev, modes_dev, 1)
    spectral_kernel = jnp.einsum(
        "esz,pzm->sepm", third_core_local, column_mode_core, precision=highest_accuracy
    )
    kernel_re = spectral_kernel[:, None, :, 0, :]
    kernel_im = spectral_kernel[:, None, :, 1, :]
    grad_re = spec_grad[:, :, None, 0, :]
    grad_im = spec_grad[:, :, None, 1, :]
    grad_inner = jnp.stack(
        [grad_re * kernel_re + grad_im * kernel_im, grad_im * kernel_re - grad_re * kernel_im],
        axis=3,
    )
    lead_part = jnp.einsum("ia,kiqy->kaqy", first_local, spec_in, precision=highest_accuracy)
    lead_grad = jnp.einsum("aob,kobqy->kaqy", second_local, grad_inner, precision=highest_accuracy)
    lead_part, lead_grad = lax.psum((lead_part, lead_grad), "chan")
    inner = jnp.einsum("aob,kaqy->kobqy", second_local, lead_part, precision=highest_accuracy)
    inner_re = inner[:, :, :, 0, :]
    inner_im = inner[:, :, :, 1, :]
    out_re = jnp.sum(inner_re * kernel_re - inner_im * kernel_im, axis=2)
    out_im = jnp.sum(inner_re * kernel_im + inner_im * kernel_re, axis=2)
    spec_out = jnp.stack([out_re, out_im], axis=2).astype(jnp.bfloat16)
    spec_back = jnp.einsum(
        "ia,kaqy->kiqy", first_local, lead_grad, precision=highest_accuracy
    ).astype(jnp.bfloat16)
    part_first = jnp.einsum("kiqy,kaqy->ia", spec_in, lead_grad, precision=highest_accuracy)
    part_second = jnp.einsum("kaqy,kobqy->aob", lead_part, grad_inner, precision=highest_accuracy)
    kernel_grad_re = jnp.sum(grad_re * inner_re + grad_im * inner_im, axis=1)
    kernel_grad_im = jnp.sum(grad_im * inner_re - grad_re * inner_im, axis=1)
    spectral_kernel_gradient = jnp.stack([kernel_grad_re, kernel_grad_im], axis=2)
    third_core_part = jnp.einsum(
        "jmlt,lct->mjc", spectral_kernel_gradient, column_mode_core, precision=highest_accuracy
    )
    fourth_core_part = jnp.einsum(
        "xcer,cxj->ejr", spectral_kernel_gradient, third_core_local, precision=highest_accuracy
    )
    first_reduced, second_reduced = lax.psum((part_first, part_second), "grid")
    sum_first, sum_second = (
        lax.all_gather(first_reduced, "chan", axis=0, tiled=True),
        lax.all_gather(second_reduced, "chan", axis=1, tiled=True),
    )
    third_reduced = lax.psum(third_core_part, "chan")
    sum_third = lax.all_gather(third_reduced, "grid", axis=1, tiled=True)
    sum_fourth = lax.psum(fourth_core_part, ("grid", "chan"))
    inverse_tables = own_tables.transpose(2, 3, 0, 1)
    tables = inverse_tables
    first_add = jnp.einsum(
        "hpkq,koqy->ohpy",
        tables,
        lax.all_gather(spec_out, "grid", axis=0, tiled=True),
        preferred_element_type=jnp.float32,
    )
    second_add = jnp.einsum(
        "hpkq,koqy->ohpy",
        tables,
        lax.all_gather(spec_back, "grid", axis=0, tiled=True),
        preferred_element_type=jnp.float32,
    )
    plain = base.transpose(1, 2, 0)
    weighted = (plain * weight_c.astype(jnp.bfloat16)[None, :, None]).reshape(
        2 * MODES_Y, GRID_SIDE
    )
    plain = plain.reshape(2 * MODES_Y, GRID_SIDE)

    def to_grid(rows, table):
        flat = rows.astype(jnp.bfloat16).reshape(chan_dev * rows_dev, 2 * MODES_Y)
        product = jnp.dot(flat, table, preferred_element_type=jnp.float32) * (1.0 / GRID_SIDE)
        return product.astype(jnp.bfloat16).reshape(chan_dev, rows_dev, GRID_SIDE)

    output_field = to_grid(first_add, weighted)
    input_grad = to_grid(second_add, plain)
    scale = 1.0 / MODES_X
    return (
        output_field,
        input_grad,
        sum_first * scale,
        sum_second * scale,
        sum_third * scale,
        sum_fourth * scale,
    )


def solution(mesh):
    placed = (P("chan", "grid", None), P("chan", "grid", None), P(), P(), P(), P())
    return jax.shard_map(
        local,
        mesh=mesh,
        in_specs=placed,
        out_specs=(P("chan", "grid", None), P("chan", "grid", None), P(), P(), P(), P()),
        check_vma=False,
    )
```

profile of v0, /device:TPU:0, one launch (start us, length us, event | category | flops | bytes accessed | tf_op | source)
XLA Modules:
  0.0 714.0 jit_solution(13766676231940642104)
XLA Ops:
  7.9 2.0 fusion.38
  9.9 2.0 cosine_convert_fusion
  11.9 0.9 fusion.73
  13.1 8.2 %fusion.21 = bf16[32,8,64,128]{3,1,2,0:T(8,128)(2,1)S(1)} fusion(bf16[1024,256]{0,1:T(8,128)(2,1)S(1)} %bitcast.243, bf16[8192,1024]{1,0:T(8,128)(2,1)} %bitcast.246), kind=kOutput, calls=%fused_computation.34 | convolution fusion | flops 4297064448 | bytes 21495808 | tf_op jit(solution)/shard_map/dot_general | solution.py:49
  21.3 1.2 copy.194
  22.5 2.7 copy.136
  25.2 8.4 %fusion.20 = bf16[32,8,64,128]{3,1,2,0:T(8,128)(2,1)S(1)} fusion(bf16[1024,256]{0,1:T(8,128)(2,1)S(1)} %bitcast.244, bf16[8192,1024]{1,0:T(8,128)(2,1)} %bitcast.247), kind=kOutput, calls=%fused_computation.33 | convolution fusion | flops 4297064448 | bytes 21495808 | tf_op jit(solution)/shard_map/dot_general | solution.py:49
  33.6 1.2 copy.193
  34.8 2.7 copy.135
  37.6 0.6 copy-done.14
  38.2 7.4 %fusion.5 = f32[128,2,64,2,128]{0,4,3,2,1:T(8,128)} fusion(bf16[1,64,128,2,128]{2,4,3,1,0:T(8,128)(2,1)S(1)} %copy.136, bf16[1,64,128,2,128]{2,4,3,1,0:T(8,128)(2,1)S(1)} %copy.135, bf16[128,1,128,2]{2,0,3,1:T(8,128)(2,1)S(1)} %get-tuple-element.59, bf16[128,1,128,2]{2,0,3,1:T(8,128)(2,1)S(1)} %get-tuple-element.58), kind=kOutput, calls=%fused_computation.22 | convolution fusion | flops 2164523008 | bytes 25296896 | tf_op jit(solution)/shard_map/kphq,fchqy->kfcpy/dot_general | solution.py:62
  45.7 16.4 %copy.137 = f32[128,2,64,2,128]{4,2,3,1,0:T(8,128)} copy(f32[128,2,64,2,128]{0,4,3,2,1:T(8,128)} %fusion.5) | data formatting | bytes 33554432 | tf_op jit(solution)/shard_map/kphq,fchqy->kfcpy/transpose | solution.py:62
  62.2 0.8 copy-done.19
  63.7 0.8 constant_dynamic-slice_fusion
  64.5 280.8 %reduce-scatter.2.cloned.1.call-done = f32[16,2,64,2,128]{4,2,3,1,0:T(8,128)} async-done(((f32[128,2,64,2,128]{4,2,3,1,0:T(8,128)}), f32[16,2,64,2,128]{4,2,3,1,0:T(8,128)}) %reduce-scatter.2.cloned.1.call-update) | async-done | bytes 2097168 | tf_op jit(solution)/shard_map/reduce_scatter | solution.py:61
  345.3 1.3 fusion.25
  346.7 2.5 multiply_add_fusion
  349.3 10.2 %fusion.23 = f32[16,16,2,128]{3,1,2,0:T(8,128)} fusion(f32[16,64,16,1,128]{4,1,2,3,0:T(8,128)S(1)} %get-tuple-element.51, f32[16,64,16,1,128]{4,1,2,3,0:T(8,128)S(1)} %get-tuple-element.50, f32[16,64,16]{1,2,0:T(8,128)S(1)} %copy-done.11), kind=kOutput, calls=%fused_computation.39 | convolution fusion | flops 809500672 | bytes 17104896 | tf_op jit(solution)/shard_map/aob,kobqy->kaqy/dot_general | solution.py:85
  359.5 1.4 convolution_bitcast_fusion.1
  361.0 32.7 %all-reduce.6.cloned.1.call-done = (f32[16,16,2,128]{3,1,2,0:T(8,128)}, f32[16,16,2,128]{3,1,2,0:T(8,128)}) async-done(((f32[16,16,2,128]{3,1,2,0:T(8,128)}, f32[16,16,2,128]{3,1,2,0:T(8,128)}), (f32[16,16,2,128]{3,1,2,0:T(8,128)}, f32[16,16,2,128]{3,1,2,0:T(8,128)})) %all-reduce.6.cloned.1.call-update) | async-done | bytes 524304 | tf_op jit(solution)/shard_map/psum | solution.py:86
  393.7 23.0 %fusion.24 = f32[16,64,16]{1,0,2:T(8,128)} fusion(f32[16,64,16,1,128]{4,1,2,3,0:T(8,128)} %copy-done.3, f32[16,64,16,1,128]{4,1,2,3,0:T(8,128)} %copy-done.2, f32[16,16,2,128]{3,1,2,0:T(8,128)} %get-tuple-element.48), kind=kOutput, calls=%fused_computation.41 | convolution fusion | flops 809500672 | bytes 17104896 | tf_op jit(solution)/shard_map/kaqy,kobqy->aob/dot_general | solution.py:97
  416.8 2.8 fusion.22
  419.7 8.8 %all-gather.4.cloned.1.call-start = ((), (), s32[]{:S(2)}) async-start(), calls=%async_computation.2 | async-start | bytes 4718592 | tf_op jit(solution)/shard_map/all_gather | solution.py:120
  428.5 14.8 %convolution_bitcast_fusion = f32[16,64,16,2,128]{4,1,2,3,0:T(8,128)S(1)} fusion(f32[16,16,2,128]{3,1,2,0:T(8,128)S(1)} %copy-done.8, f32[16,64,16]{1,2,0:T(8,128)} %constant_dynamic-slice_fusion), kind=kOutput, calls=%fused_computation.7 | convolution fusion | flops 805306368 | bytes 17104896 | tf_op jit(solution)/shard_map/aob,kaqy->kobqy/dot_general | solution.py:87
  443.3 7.0 add_reduce_fusion
  450.7 0.8 pad_maximum_fusion.8
  451.5 1.0 broadcast_multiply_fusion.2
  452.5 1.0 copy.148
  453.6 1.2 copy.154
  454.8 1.9 convolution_bitcast_fusion.5
  456.7 21.8 %psum.44 = f32[64,16]{0,1:T(8,128)S(1)} all-reduce(f32[64,16]{0,1:T(8,128)S(1)} %convolution_bitcast_fusion.5), channel_id=1, replica_groups=mesh['grid'=8,'chan'=4] {'grid'}, use_global_device_ids=true, to_apply=%region_5.6 | all-reduce | flops 1024 | bytes 8192 | tf_op jit(solution)/shard_map/psum | solution.py:107
  478.5 5.2 all-gather
  483.7 0.7 reshape.349
  484.4 1.3 convolution_bitcast_fusion.3
  485.7 12.1 %psum.46 = f32[16,16,16]{2,0,1:T(8,128)S(1)} all-reduce(f32[16,16,16]{2,0,1:T(8,128)S(1)} %convolution_bitcast_fusion.3), channel_id=1, replica_groups=mesh['grid'=8,'chan'=4] {'chan'}, use_global_device_ids=true, to_apply=%region_9.10 | all-reduce | flops 4096 | bytes 32768 | tf_op jit(solution)/shard_map/psum | solution.py:112
  497.9 36.2 %all_gather.19 = f32[16,128,16]{2,0,1:T(8,128)S(1)} all-gather(f32[16,16,16]{2,0,1:T(8,128)S(1)} %psum.46), channel_id=1, replica_groups=mesh['grid'=8,'chan'=4] {'grid'}, dimensions={1}, use_global_device_ids=true | all-gather | bytes 147456 | tf_op jit(solution)/shard_map/all_gather | solution.py:113
  534.1 1.1 copy.161
  535.8 39.6 %psum.47 = f32[2,16,128]{2,1,0:T(8,128)S(1)} all-reduce(f32[2,16,128]{2,1,0:T(8,128)S(1)} %convolution_bitcast_fusion.4), channel_id=1, replica_groups=mesh['grid'=8,'chan'=4] {'grid','chan'}, use_global_device_ids=true, to_apply=%region_10.11 | all-reduce | flops 4096 | bytes 32768 | tf_op jit(solution)/shard_map/psum | solution.py:114
  576.0 1.2 copy.157
  577.2 16.9 %all_gather.18 = f32[16,256,16]{2,0,1:T(8,128)S(1)} all-gather(f32[16,64,16]{2,0,1:T(8,128)S(1)} %copy.157), channel_id=1, replica_groups=mesh['grid'=8,'chan'=4] {'chan'}, dimensions={1}, use_global_device_ids=true | all-gather | bytes 327680 | tf_op jit(solution)/shard_map/all_gather | solution.py:110
  594.3 1.7 copy.160
  596.0 7.5 %fusion.6 = bf16[64,128,2,128]{1,3,2,0:T(8,128)(2,1)S(1)} fusion(bf16[128,64,2,128,1]{3,1,2,0,4:T(8,128)(2,1)} %bitcast.232, bf16[128,1,128,2]{2,0,3,1:T(8,128)(2,1)S(1)} %copy-done.17, bf16[128,1,128,2]{2,0,3,1:T(8,128)(2,1)S(1)} %copy-done.15), kind=kOutput, calls=%fused_computation.23 | convolution fusion | flops 1075904512 | bytes 8519680 | tf_op jit(solution)/shard_map/hpkq,koqy->ohpy/dot_general | solution.py:123
  603.5 4.7 copy.153
  608.2 39.3 %all-gather.4.cloned.1.call-done = bf16[128,64,2,128]{3,0,2,1:T(8,128)(2,1)} async-done(((bf16[16,64,2,128]{3,0,2,1:T(8,128)(2,1)}), bf16[128,64,2,128]{3,0,2,1:T(8,128)(2,1)}) %all-gather.4.cloned.1.call-update) | async-done | bytes 4194320 | tf_op jit(solution)/shard_map/all_gather | solution.py:120
  647.5 3.5 fusion.7
  651.0 4.8 copy.147
  655.9 25.6 %multiply_convert_fusion = bf16[8192,1024]{1,0:T(8,128)(2,1)} fusion(bf16[256,1024]{1,0:T(8,128)(2,1)S(1)} %bitcast.242, bf16[32,8,64,128]{3,2,1,0:T(8,128)(2,1)} %bitcast.233), kind=kOutput, calls=%fused_computation | convolution fusion | flops 4311744512 | bytes 21495808 | tf_op jit(solution)/shard_map/dot_general | solution.py:137
  681.5 25.7 %multiply_convert_fusion.1 = bf16[8192,1024]{1,0:T(8,128)(2,1)} fusion(bf16[256,1024]{1,0:T(8,128)(2,1)S(1)} %bitcast.241, bf16[32,8,64,128]{3,2,1,0:T(8,128)(2,1)} %bitcast.234), kind=kOutput, calls=%fused_computation.1 | convolution fusion | flops 4311744512 | bytes 21495808 | tf_op jit(solution)/shard_map/dot_general | solution.py:137
  (76 shorter events, 3.8 us)
Async XLA Ops:
  7.2 56.5 %copy-start = (f32[16,256,16]{1,2,0:T(8,128)S(1)}, f32[16,256,16]{1,2,0:T(8,128)}, u32[]{:S(2)}) copy-start(f32[16,256,16]{1,2,0:T(8,128)} %param.9) | copy-start | bytes 786436
  7.2 338.1 %reduce-scatter.2.cloned.1.call-start = ((), (), s32[]{:S(2)}) async-start(), calls=%async_computation.1 | async-start | bytes 18874368 | tf_op jit(solution)/shard_map/reduce_scatter | solution.py:61
  9.9 2.0 copy-start.5
  11.9 1.0 copy-start.7
  37.6 0.6 copy-start.14
  37.6 0.7 copy-start.16
  62.1 0.9 copy-start.19
  62.1 0.9 copy-start.21
  62.1 331.6 %all-reduce.6.cloned.1.call-start = ((), (), s32[]{:S(2)}) async-start(), calls=%async_computation.5 | async-start | bytes 1048576 | tf_op jit(solution)/shard_map/psum | solution.py:86
  63.7 285.5 %copy-start.9 = (f32[16,16,128]{2,1,0:T(8,128)}, f32[16,16,128]{2,1,0:T(8,128)S(1)}, u32[]{:S(2)}) copy-start(f32[16,16,128]{2,1,0:T(8,128)S(1)} %copy.143) | copy-start | bytes 393220
  346.7 2.6 copy-start.11
  349.2 10.3 %copy-start.2 = (f32[16,64,16,1,128]{4,1,2,3,0:T(8,128)}, f32[16,64,16,1,128]{4,1,2,3,0:T(8,128)S(1)}, u32[]{:S(2)}) copy-start(f32[16,64,16,1,128]{4,1,2,3,0:T(8,128)S(1)} %get-tuple-element.50) | copy-start | bytes 25165828
  349.2 10.2 %copy-start.3 = (f32[16,64,16,1,128]{4,1,2,3,0:T(8,128)}, f32[16,64,16,1,128]{4,1,2,3,0:T(8,128)S(1)}, u32[]{:S(2)}) copy-start(f32[16,64,16,1,128]{4,1,2,3,0:T(8,128)S(1)} %get-tuple-element.51) | copy-start | bytes 25165828
  349.3 10.2 %copy-start.4 = (f32[16,2,64,2,128]{4,2,3,1,0:T(8,128)S(1)}, f32[16,2,64,2,128]{4,2,3,1,0:T(8,128)}, u32[]{:S(2)}) copy-start(f32[16,2,64,2,128]{4,2,3,1,0:T(8,128)} %reduce-scatter.2.cloned.1.call-done) | copy-start | bytes 6291460
  349.3 10.2 %copy-start.22 = (f32[256,16]{0,1:T(8,128)S(1)}, f32[256,16]{0,1:T(8,128)}, u32[]{:S(2)}) copy-start(f32[256,16]{0,1:T(8,128)} %param.8) | copy-start | bytes 49156
  360.9 215.1 %all-reduce.4.cloned.1.call-start = ((), (), s32[]{:S(2)}) async-start(), calls=%async_computation.4 | async-start | bytes 262144 | tf_op jit(solution)/shard_map/psum | solution.py:107
  393.7 34.8 %copy-start.8 = (f32[16,16,2,128]{3,1,2,0:T(8,128)S(1)}, f32[16,16,2,128]{3,1,2,0:T(8,128)}, u32[]{:S(2)}) copy-start(f32[16,16,2,128]{3,1,2,0:T(8,128)} %get-tuple-element.48) | copy-start | bytes 786436
  416.8 179.2 %all-gather.6.cloned.1.call-start = ((), (), s32[]{:S(2)}) async-start(), calls=%async_computation.3 | async-start | bytes 4718592 | tf_op jit(solution)/shard_map/all_gather | solution.py:126
  419.7 227.9 %all-gather.4.cloned.1.call-start = ((), (), s32[]{:S(2)}) async-start(), calls=%async_computation.2 | async-start | bytes 4718592 | tf_op jit(solution)/shard_map/all_gather | solution.py:120
  428.5 14.8 %copy-start.10 = (f32[16,16,128]{2,1,0:T(8,128)S(1)}, f32[16,16,128]{2,1,0:T(8,128)}, u32[]{:S(2)}) copy-start(f32[16,16,128]{2,1,0:T(8,128)} %copy-done.9) | copy-start | bytes 393220
  443.3 8.3 %copy-start.6 = (bf16[1024,1,128]{2,0,1:T(8,128)(2,1)S(1)}, bf16[1024,1,128]{2,0,1:T(8,128)(2,1)}, u32[]{:S(2)}) copy-start(bf16[1024,1,128]{2,0,1:T(8,128)(2,1)} %copy-done.5) | copy-start | bytes 786436
  450.3 84.9 %copy-start.12 = (f32[16,16,128]{2,1,0:T(8,128)S(1)}, f32[16,16,128]{2,1,0:T(8,128)}, u32[]{:S(2)}) copy-start(f32[16,16,128]{2,1,0:T(8,128)} %get-tuple-element.42) | copy-start | bytes 393220
  450.3 84.9 %copy-start.13 = (f32[16,16,128]{2,1,0:T(8,128)S(1)}, f32[16,16,128]{2,1,0:T(8,128)}, u32[]{:S(2)}) copy-start(f32[16,16,128]{2,1,0:T(8,128)} %get-tuple-element.43) | copy-start | bytes 393220
  450.3 84.9 %copy-start.20 = (f32[16,128,16]{1,2,0:T(8,128)S(1)}, f32[16,128,16]{1,2,0:T(8,128)}, u32[]{:S(2)}) copy-start(f32[16,128,16]{1,2,0:T(8,128)} %param.10) | copy-start | bytes 393220
  456.7 139.3 %copy-start.15 = (bf16[128,1,128,2]{2,0,3,1:T(8,128)(2,1)S(1)}, bf16[128,1,128,2]{2,0,3,1:T(8,128)(2,1)}, u32[]{:S(2)}) copy-start(bf16[128,1,128,2]{2,0,3,1:T(8,128)(2,1)} %copy-done.14) | copy-start | bytes 196612
  456.7 139.3 %copy-start.17 = (bf16[128,1,128,2]{2,0,3,1:T(8,128)(2,1)S(1)}, bf16[128,1,128,2]{2,0,3,1:T(8,128)(2,1)}, u32[]{:S(2)}) copy-start(bf16[128,1,128,2]{2,0,3,1:T(8,128)(2,1)} %copy-done.16) | copy-start | bytes 196612
  655.9 25.6 %copy-start.18 = (bf16[2,128,1024]{2,1,0:T(8,128)(2,1)S(1)}, bf16[2,128,1024]{2,1,0:T(8,128)(2,1)}, u32[]{:S(2)}) copy-start(bf16[2,128,1024]{2,1,0:T(8,128)(2,1)} %copy.148) | copy-start | bytes 1572868
  681.5 25.7 %copy-start.1 = (f32[16,256,16]{1,2,0:T(8,128)S(1)}, f32[16,256,16]{1,2,0:T(8,128)}, u32[]{:S(2)}) copy-start(f32[16,256,16]{1,2,0:T(8,128)} %param.9) | copy-start | bytes 786436
Sparse Core Ops, SparseCore 0:
  62.3 282.9 reduce-scatter.1
  361.0 32.6 all-reduce.5
  416.9 70.5 all-reduce.3
  490.1 81.8 all-gather.5
  574.4 73.0 all-gather.3
where the time goes:
time: 722 us; the launch traced here: 714 us
  waiting for transfers between devices  353 us (49%)
  matrix products  143 us (20%)
  blocking collectives  132 us (18%)
  local copies, waits for them, and re-layouts  43.8 us (6%)
  other arithmetic  19.1 us (3%)
  between operations  14.5 us (2%)
  starting transfers between devices  8.95 us (1%)
    reduce_scatter x1, waiting for transfers between devices, local(): lax.psum_scatter(jnp.einsum('kphq,fchqy->kfcpy', tables, both_rows, prefe...  281 us
    dot_general x2, matrix products, to_grid(): jnp.dot(flat, table, preferred_element_type=jnp.float32) * (1.0 / GRID_SIDE)  51.3 us
    psum x1, blocking collectives, local(): sum_fourth = lax.psum(fourth_core_part, ('grid', 'chan'))  39.6 us
    all_gather x1, waiting for transfers between devices, local(): lax.all_gather(spec_out, 'grid', axis=0, tiled=True)  39.3 us
    all_gather x1, blocking collectives, local(): sum_third = lax.all_gather(third_reduced, 'grid', axis=1, tiled=True)  36.2 us
    psum x1, waiting for transfers between devices, local(): lead_part, lead_grad = lax.psum((lead_part, lead_grad), 'chan')  32.7 us
    dot_general x1, matrix products, local(): jnp.einsum('kaqy,kobqy->aob', lead_part, grad_inner, precision=highest_ac...  23 us
    psum x1, blocking collectives, local(): first_reduced, second_reduced = lax.psum((part_first, part_second), 'grid')  21.8 us
  transfers between devices with their start and end apart: 5, of which 3 were waited for; matrix products, arithmetic and copies ran while one was open for 7% of the time, Pallas kernels for 0%

commit v1 on v0

v1 whole, which is shorter than its diff:
```python
import math

import jax
import jax.numpy as jnp
import numpy as np
from jax import lax
from jax.experimental import pallas as pl
from jax.experimental.pallas import tpu as pltpu
from jax.sharding import PartitionSpec as P

F32 = jnp.float32
BF16 = jnp.bfloat16
HI = lax.Precision.HIGHEST
STEP = 16


def params(mib=48):
    return pltpu.CompilerParams(vmem_limit_bytes=mib * 2**20)


def dot(a, b, precision=None):
    return jnp.dot(a, b, preferred_element_type=F32, precision=precision)


def dot_nt(a, b, precision=None):
    return lax.dot_general(
        a, b, (((1,), (1,)), ((), ())), preferred_element_type=F32, precision=precision
    )


def dot_tn(a, b, precision=None):
    return lax.dot_general(
        a, b, (((0,), (0,)), ((), ())), preferred_element_type=F32, precision=precision
    )


def width_table(side, modes_y):
    phase = np.arange(side)[:, None] * np.arange(modes_y)[None, :] % side
    angle = phase.astype(np.float32) * np.float32(2.0 * math.pi / side)
    return np.concatenate([np.cos(angle), -np.sin(angle)], axis=1).astype(BF16)


def turn_table(side, modes_x):
    kx = np.arange(modes_x)
    freq = np.where(kx < modes_x // 2, kx, side - modes_x + kx)
    phase = freq[:, None] * np.arange(side)[None, :] % side
    angle = phase.astype(np.float32) * np.float32(2.0 * math.pi / side)
    return np.stack([np.cos(angle), np.sin(angle)]).astype(BF16)


def forward_turn(cs, block):
    x = dot(cs, block)
    n, m = x.shape[0] // 2, x.shape[1] // 2
    return x[:n, :m] + x[n:, m:], x[:n, m:] - x[n:, :m]


def inverse_turn(cs, block):
    x = dot(cs, block)
    n, m = x.shape[0] // 2, x.shape[1] // 2
    return x[:n, :m] - x[n:, m:], x[:n, m:] + x[n:, :m]


def spread(values, rows):
    n = values.shape[1]
    lane = lax.broadcasted_iota(jnp.int32, (n, n * STEP), 1)
    row = lax.broadcasted_iota(jnp.int32, (n, n * STEP), 0)
    wide = dot(values, (lane // STEP == row).astype(BF16))
    at = lax.broadcasted_iota(jnp.int32, (STEP, n * STEP), 1) % STEP
    unit = (at == lax.broadcasted_iota(jnp.int32, (STEP, n * STEP), 0)).astype(F32)
    return (wide[:, None, :] * unit[None]).reshape(rows * STEP, n * STEP).astype(BF16)


def lead_kernel(first_t, table, cs, field, modes, lead, kron, rows):
    step = pl.program_id(0)
    chan, _, side = field.shape
    rank = first_t.shape[0]
    wide = table.shape[1]

    @pl.when(step == 0)
    def _():
        kron[...] = spread(first_t[...], rank)

    product = dot(field[...].reshape(chan * STEP, side), table[...]).astype(BF16)
    modes[...] = product.reshape(chan, STEP, wide)
    mixed = dot(kron[...], product)
    rows[:, pl.ds(pl.multiple_of(step * STEP, STEP), STEP), :] = mixed.reshape(
        rank, STEP, wide
    ).astype(BF16)

    @pl.when(step == pl.num_programs(0) - 1)
    def _():
        half = wide // 2
        for a in range(rank):
            re, im = forward_turn(cs[...], rows[a])
            lead[a, :, :half] = re * (1.0 / side)
            lead[a, :, half:] = im * (1.0 / side)


def grad_kernel(table, cs, weight, field, spectrum, held):
    chan, rows, side = field.shape
    wide = table.shape[1]
    half = wide // 2
    product = dot(field[...].reshape(chan * rows, side), table[...]).astype(BF16)
    for c in range(chan):
        re, im = forward_turn(cs[...], product[c * rows : (c + 1) * rows])
        held[c, :, :half] = re * weight[:, :half]
        held[c, :, half:] = im * weight[:, half:]
    spectrum[...] = jnp.swapaxes(held[...], 0, 1).astype(BF16)


def back_kernel(second_ba, kernel, spectrum, out, held):
    rank_b = kernel.shape[1]
    rank_a = second_ba.shape[0] // rank_b
    half = kernel.shape[2] // 2

    def body(k, carry):
        g = dot(second_ba[...], spectrum[k])
        kr = kernel[k]
        re = jnp.zeros((rank_a, half), F32)
        im = jnp.zeros((rank_a, half), F32)
        for b in range(rank_b):
            gre = g[b * rank_a : (b + 1) * rank_a, :half]
            gim = g[b * rank_a : (b + 1) * rank_a, half:]
            kre, kim = kr[b : b + 1, :half], kr[b : b + 1, half:]
            re += gre * kre + gim * kim
            im += gim * kre - gre * kim
        held[k, :, :half] = re
        held[k, :, half:] = im
        return carry

    lax.fori_loop(0, STEP, body, 0, unroll=2)
    out[...] = jnp.swapaxes(held[...], 0, 1)


def mix_kernel(
    lead, kernel, spectrum, second_ab, second_t, third, column,
    out, part_second, part_third, part_fourth,
    lead_k, outer, out_k, kernel_grad,
):
    rank_a = lead.shape[0]
    rank_b = kernel.shape[1]
    half = kernel.shape[2] // 2
    lead_k[...] = jnp.swapaxes(lead[...], 0, 1)

    @pl.when(pl.program_id(0) == 0)
    def _():
        part_second[...] = jnp.zeros_like(part_second)
        part_fourth[...] = jnp.zeros_like(part_fourth)

    def body(k, carry):
        spec = spectrum[k]
        g = dot(second_ab[...], spec)
        kr, ld = kernel[k], lead_k[k]
        kre, kim = kr[:, :half], kr[:, half:]
        re = jnp.zeros((rank_b, half), F32)
        im = jnp.zeros((rank_b, half), F32)
        for a in range(rank_a):
            rows = slice(a * rank_b, (a + 1) * rank_b)
            lre, lim = ld[a : a + 1, :half], ld[a : a + 1, half:]
            outer[rows, :half] = (kre * lre - kim * lim).astype(BF16)
            outer[rows, half:] = (kre * lim + kim * lre).astype(BF16)
            gre, gim = g[rows, :half], g[rows, half:]
            re += gre * lre + gim * lim
            im += gim * lre - gre * lim
        at = pl.ds(pl.multiple_of(k * rank_b, rank_b), rank_b)
        kernel_grad[at, :half] = re
        kernel_grad[at, half:] = im
        out_k[k] = dot(second_t[...], outer[...])
        part_second[...] += dot_nt(spec, outer[...])
        return carry

    lax.fori_loop(0, STEP, body, 0, unroll=2)
    out[...] = jnp.swapaxes(out_k[...], 0, 1).astype(BF16)
    part_third[0] = dot_nt(column[...], kernel_grad[...], HI)
    part_fourth[...] += dot_tn(third[...], kernel_grad[...], HI)


def field_kernel(cs, table, spectrum, out, rows):
    chan = spectrum.shape[0]
    n = out.shape[1]
    half = table.shape[0] // 2
    lane = lax.broadcasted_iota(jnp.int32, (n, half), 1)
    scale = jnp.where(lane == 0, 1.0, 2.0) * (1.0 / table.shape[1])
    for c in range(chan):
        re, im = inverse_turn(cs[...], spectrum[c])
        rows[c * n : (c + 1) * n, :half] = (re * scale).astype(BF16)
        rows[c * n : (c + 1) * n, half:] = (im * scale).astype(BF16)
        out[c] = dot(rows[c * n : (c + 1) * n, :], table[...]).astype(BF16)


def first_kernel(cs, lead_grad, modes, rows, part_first, total):
    step = pl.program_id(0)
    rank, n, wide = rows.shape
    chan = modes.shape[0]
    half = wide // 2

    @pl.when(step == 0)
    def _():
        total[...] = jnp.zeros_like(total)
        for a in range(rank):
            re, im = inverse_turn(cs[...], lead_grad[a].astype(BF16))
            rows[a, :, :half] = re.astype(BF16)
            rows[a, :, half:] = im.astype(BF16)

    at = pl.ds(pl.multiple_of(step * STEP, STEP), STEP)
    block = rows[:, at, :].reshape(rank * STEP, wide)
    total[...] += dot_nt(modes[...].reshape(chan * STEP, wide), block)

    @pl.when(step == pl.num_programs(0) - 1)
    def _():
        shape = (STEP, rank * STEP)
        unit = lax.broadcasted_iota(jnp.int32, shape, 1) % STEP == lax.broadcasted_iota(
            jnp.int32, shape, 0
        )
        kept = total[...].reshape(chan, STEP, rank * STEP) * unit.astype(F32)[None]
        lane = lax.broadcasted_iota(jnp.int32, (rank, rank * STEP), 1)
        row = lax.broadcasted_iota(jnp.int32, (rank, rank * STEP), 0)
        pick = (lane // STEP == row).astype(F32)
        part_first[...] = dot_nt(pick, jnp.sum(kept, axis=1), HI)


def input_kernel(first, table, rows, out, kron):
    rank, _, wide = rows.shape
    chan, _, side = out.shape

    @pl.when(pl.program_id(0) == 0)
    def _():
        kron[...] = spread(first[...], chan)

    block = dot(kron[...], rows[...].reshape(rank * STEP, wide)) * (1.0 / side)
    out[...] = dot(block.astype(BF16), table[...]).astype(BF16).reshape(out.shape)


def whole(shape):
    return pl.BlockSpec(shape, lambda i: (0,) * len(shape))


def sum_all(x):
    return lax.psum(x, ("grid", "chan"))


def local(input_field, out_cotangent, core_first, core_second, core_third, column_mode_core):
    grid_count = lax.axis_size("grid")
    grid_index = lax.axis_index("grid")
    chan_index = lax.axis_index("chan")
    chan, rows, side = input_field.shape
    channels, rank_a = core_first.shape
    rank_b, modes_x, rank_d = core_third.shape
    modes_y = column_mode_core.shape[2]
    wide = 2 * modes_y

    table_np = width_table(side, modes_y)
    table = jnp.asarray(table_np)
    table_t = jnp.asarray(np.ascontiguousarray(table_np.T))
    turns = turn_table(side, modes_x).reshape(2, modes_x, grid_count, rows)
    forward = np.ascontiguousarray(turns.transpose(2, 0, 1, 3)).reshape(
        grid_count, 2 * modes_x, rows
    )
    backward = np.ascontiguousarray(turns.transpose(2, 0, 3, 1)).reshape(
        grid_count, 2 * rows, modes_x
    )
    cs = lax.dynamic_index_in_dim(jnp.asarray(forward), grid_index, 0, keepdims=False)
    cs_t = lax.dynamic_index_in_dim(jnp.asarray(backward), grid_index, 0, keepdims=False)
    weight_c = np.where(np.arange(wide) % modes_y == 0, 1.0, 2.0).astype(np.float32)
    weight = jnp.asarray((weight_c / side)[None, :])

    first_local = lax.dynamic_slice_in_dim(core_first, chan_index * chan, chan, 0)
    second_local = lax.dynamic_slice_in_dim(core_second, chan_index * chan, chan, 1)
    first_bf = first_local.astype(BF16)
    second_bf = second_local.astype(BF16)
    pairs = rank_a * rank_b
    second_ab = second_bf.transpose(0, 2, 1).reshape(pairs, chan)
    second_ba = second_bf.transpose(2, 0, 1).reshape(pairs, chan)
    second_t = second_bf.transpose(1, 0, 2).reshape(chan, pairs)
    third_rows = core_third.transpose(1, 0, 2).reshape(modes_x * rank_b, rank_d)
    column = column_mode_core.transpose(1, 0, 2).reshape(rank_d, wide)
    kernel = dot(third_rows, column, HI).reshape(modes_x, rank_b, wide)

    row_steps = rows // STEP
    mode_steps = modes_x // STEP
    chan_step = min(chan, STEP)
    out_step = min(chan, 8)

    row_modes, lead = pl.pallas_call(
        lead_kernel,
        grid=(row_steps,),
        in_specs=[
            whole((rank_a, chan)),
            whole((side, wide)),
            whole((2 * modes_x, rows)),
            pl.BlockSpec((chan, STEP, side), lambda i: (0, i, 0)),
        ],
        out_specs=[
            pl.BlockSpec((chan, STEP, wide), lambda i: (0, i, 0)),
            whole((rank_a, modes_x, wide)),
        ],
        out_shape=[
            jax.ShapeDtypeStruct((chan, rows, wide), BF16),
            jax.ShapeDtypeStruct((rank_a, modes_x, wide), F32),
        ],
        scratch_shapes=[
            pltpu.VMEM((rank_a * STEP, chan * STEP), BF16),
            pltpu.VMEM((rank_a, rows, wide), BF16),
        ],
        compiler_params=params(),
        name="lead",
    )(first_bf.T, table, cs, input_field)
    lead = sum_all(lead)

    spec_grad = pl.pallas_call(
        grad_kernel,
        grid=(chan // chan_step,),
        in_specs=[
            whole((side, wide)),
            whole((2 * modes_x, rows)),
            whole((1, wide)),
            pl.BlockSpec((chan_step, rows, side), lambda i: (i, 0, 0)),
        ],
        out_specs=pl.BlockSpec((modes_x, chan_step, wide), lambda i: (0, i, 0)),
        out_shape=jax.ShapeDtypeStruct((modes_x, chan, wide), BF16),
        scratch_shapes=[pltpu.VMEM((chan_step, modes_x, wide), F32)],
        compiler_params=params(),
        name="spec_grad",
    )(table, cs, weight, out_cotangent)

    lead_grad = pl.pallas_call(
        back_kernel,
        grid=(mode_steps,),
        in_specs=[
            whole((pairs, chan)),
            pl.BlockSpec((STEP, rank_b, wide), lambda i: (i, 0, 0)),
            pl.BlockSpec((STEP, chan, wide), lambda i: (i, 0, 0)),
        ],
        out_specs=pl.BlockSpec((rank_a, STEP, wide), lambda i: (0, i, 0)),
        out_shape=jax.ShapeDtypeStruct((rank_a, modes_x, wide), F32),
        scratch_shapes=[pltpu.VMEM((STEP, rank_a, wide), F32)],
        compiler_params=params(),
        name="lead_grad",
    )(second_ba, kernel, spec_grad)
    lead_grad = sum_all(lead_grad)

    spec_out, part_second, part_third, part_fourth = pl.pallas_call(
        mix_kernel,
        grid=(mode_steps,),
        in_specs=[
            pl.BlockSpec((rank_a, STEP, wide), lambda i: (0, i, 0)),
            pl.BlockSpec((STEP, rank_b, wide), lambda i: (i, 0, 0)),
            pl.BlockSpec((STEP, chan, wide), lambda i: (i, 0, 0)),
            whole((pairs, chan)),
            whole((chan, pairs)),
            pl.BlockSpec((STEP * rank_b, rank_d), lambda i: (i, 0)),
            whole((rank_d, wide)),
        ],
        out_specs=[
            pl.BlockSpec((chan, STEP, wide), lambda i: (0, i, 0)),
            whole((chan, pairs)),
            pl.BlockSpec((1, rank_d, STEP * rank_b), lambda i: (i, 0, 0)),
            whole((rank_d, wide)),
        ],
        out_shape=[
            jax.ShapeDtypeStruct((chan, modes_x, wide), BF16),
            jax.ShapeDtypeStruct((chan, pairs), F32),
            jax.ShapeDtypeStruct((mode_steps, rank_d, STEP * rank_b), F32),
            jax.ShapeDtypeStruct((rank_d, wide), F32),
        ],
        scratch_shapes=[
            pltpu.VMEM((STEP, rank_a, wide), F32),
            pltpu.VMEM((pairs, wide), BF16),
            pltpu.VMEM((STEP, chan, wide), F32),
            pltpu.VMEM((STEP * rank_b, wide), F32),
        ],
        compiler_params=params(),
        name="mix",
    )(lead, kernel, spec_grad, second_ab, second_t, third_rows, column)

    back_rows, part_first = pl.pallas_call(
        first_kernel,
        grid=(row_steps,),
        in_specs=[
            whole((2 * rows, modes_x)),
            whole((rank_a, modes_x, wide)),
            pl.BlockSpec((chan, STEP, wide), lambda i: (0, i, 0)),
        ],
        out_specs=[whole((rank_a, rows, wide)), whole((rank_a, chan))],
        out_shape=[
            jax.ShapeDtypeStruct((rank_a, rows, wide), BF16),
            jax.ShapeDtypeStruct((rank_a, chan), F32),
        ],
        scratch_shapes=[pltpu.VMEM((chan * STEP, rank_a * STEP), F32)],
        compiler_params=params(),
        name="first",
    )(cs_t, lead_grad, row_modes)

    first_wide = lax.dynamic_update_slice(
        jnp.zeros((rank_a, channels), F32), part_first * (1.0 / side), (0, chan_index * chan)
    )
    second_wide = lax.dynamic_update_slice(
        jnp.zeros((channels, pairs), F32), part_second, (chan_index * chan, 0)
    )
    sizes = [first_wide.size, second_wide.size, part_third.size, part_fourth.size]
    packed = jnp.concatenate(
        [v.reshape(-1, wide) for v in (first_wide, second_wide, part_third, part_fourth)]
    )
    packed = sum_all(packed) * (1.0 / modes_x)
    cuts = np.cumsum([0] + [s // wide for s in sizes])
    one, two, three, four = (packed[cuts[n] : cuts[n + 1]] for n in range(4))
    grad_first = one.reshape(rank_a, channels).T
    grad_second = two.reshape(channels, rank_a, rank_b).transpose(1, 0, 2)
    grad_third = (
        three.reshape(mode_steps, rank_d, STEP, rank_b)
        .transpose(3, 0, 2, 1)
        .reshape(rank_b, modes_x, rank_d)
    )
    grad_fourth = four.reshape(rank_d, 2, modes_y).transpose(1, 0, 2)

    output_field = pl.pallas_call(
        field_kernel,
        grid=(chan // out_step,),
        in_specs=[
            whole((2 * rows, modes_x)),
            whole((wide, side)),
            pl.BlockSpec((out_step, modes_x, wide), lambda i: (i, 0, 0)),
        ],
        out_specs=pl.BlockSpec((out_step, rows, side), lambda i: (i, 0, 0)),
        out_shape=jax.ShapeDtypeStruct((chan, rows, side), BF16),
        scratch_shapes=[pltpu.VMEM((out_step * rows, wide), BF16)],
        compiler_params=params(),
        name="output",
    )(cs_t, table_t, spec_out)

    input_grad = pl.pallas_call(
        input_kernel,
        grid=(row_steps,),
        in_specs=[
            whole((chan, rank_a)),
            whole((wide, side)),
            pl.BlockSpec((rank_a, STEP, wide), lambda i: (0, i, 0)),
        ],
        out_specs=pl.BlockSpec((chan, STEP, side), lambda i: (0, i, 0)),
        out_shape=jax.ShapeDtypeStruct((chan, rows, side), BF16),
        scratch_shapes=[pltpu.VMEM((chan * STEP, rank_a * STEP), BF16)],
        compiler_params=params(),
        name="input_grad",
    )(first_bf, table_t, back_rows)

    return output_field, input_grad, grad_first, grad_second, grad_third, grad_fourth


def solution(mesh):
    placed = (P("chan", "grid", None), P("chan", "grid", None), P(), P(), P(), P())
    return jax.shard_map(
        local,
        mesh=mesh,
        in_specs=placed,
        out_specs=(P("chan", "grid", None), P("chan", "grid", None), P(), P(), P(), P()),
        check_vma=False,
    )
```

time: 722 us -> 388 us (0.54); the launches traced: 714 us -> 387 us
  matrix products: 143 us -> 1.77 us
  blocking collectives: 132 us -> 0 us
  waiting for transfers between devices: 353 us -> 241 us
  Pallas kernels: 0 us -> 105 us
  local copies, waits for them, and re-layouts: 43.8 us -> 23 us
  other arithmetic: 19.1 us -> 2.41 us
  starting transfers between devices: 8.95 us -> 0.26 us
    reduce_scatter x1 -> x0, waiting for transfers between devices: 281 us -> none  [local(): lax.psum_scatter(jnp.einsum('kphq,fchqy->kfcpy', tables, both_rows, prefe...]
    psum x2, waiting for transfers between devices: 32.7 us -> 241 us  [sum_all(): return lax.psum(x, ('grid', 'chan'))]
    dot_general x16 -> x1, matrix products: 143 us -> 1.77 us  [dot(): return jnp.dot(a, b, preferred_element_type=F32, precision=precision)]
    pallas_call x0 -> x7, Pallas kernels: none -> 105 us  [the longest x1 27.6 us: local(): pl.pallas_call(mix_kernel, grid=(mode_steps,), in_specs=[pl.BlockSpec((ra...]
    psum x3 -> x0, blocking collectives: 73.5 us -> none  [the longest x1 39.6 us: local(): sum_fourth = lax.psum(fourth_core_part, ('grid', 'chan'))]
    all_gather x3 -> x0, blocking collectives: 58.3 us -> none  [the longest x1 36.2 us: local(): sum_third = lax.all_gather(third_reduced, 'grid', axis=1, tiled=True)]
    all_gather x2 -> x0, waiting for transfers between devices: 39.3 us -> none  [the longest x1 39.3 us: local(): lax.all_gather(spec_out, 'grid', axis=0, tiled=True)]
    transpose x2 -> x5, local copies, waits for them, and re-layouts: 17.7 us -> 2.9 us  [the longest x1 1.39 us: local(): third_rows = core_third.transpose(1, 0, 2).reshape(modes_x * rank_b, rank_d)]
  transfers between devices with their start and end apart: 5 -> 2, of which waited for: 3 -> 2; matrix products, arithmetic and copies ran while one was open for 7% -> 0% of each run, Pallas kernels for 0% -> 7%
where the time goes in v1:
time: 388 us; the launch traced here: 387 us
  waiting for transfers between devices  241 us (62%)
  Pallas kernels  105 us (27%)
  local copies, waits for them, and re-layouts  23 us (6%)
  between operations  14.2 us (4%)
    psum x2, waiting for transfers between devices, sum_all(): return lax.psum(x, ('grid', 'chan'))  241 us
    pallas_call x1, Pallas kernels, local(): pl.pallas_call(mix_kernel, grid=(mode_steps,), in_specs=[pl.BlockSpec((ra...  27.6 us
    pallas_call x1, Pallas kernels, local(): pl.pallas_call(field_kernel, grid=(chan // out_step,), in_specs=[whole((2...  17.1 us
    pallas_call x1, Pallas kernels, local(): pl.pallas_call(back_kernel, grid=(mode_steps,), in_specs=[whole((pairs, c...  15.1 us
    pallas_call x1, Pallas kernels, local(): pl.pallas_call(lead_kernel, grid=(row_steps,), in_specs=[whole((rank_a, c...  14.4 us
    pallas_call x1, Pallas kernels, local(): pl.pallas_call(grad_kernel, grid=(chan // chan_step,), in_specs=[whole((s...  13.7 us
    unnamed x30, local copies, waits for them, and re-layouts  13 us
    pallas_call x1, Pallas kernels, local(): pl.pallas_call(input_kernel, grid=(row_steps,), in_specs=[whole((chan, ra...  9.82 us
  transfers between devices with their start and end apart: 2, of which 2 were waited for; matrix products, arithmetic and copies ran while one was open for 0% of the time, Pallas kernels for 7%

profile of v1, /device:TPU:0, one launch (start us, length us, event | category | flops | bytes accessed | tf_op | source)
XLA Modules:
  0.0 387.3 jit_solution(11413766033074811675)
XLA Ops:
  7.2 0.0 copy-start
  7.2 0.0 all-reduce.6.cloned.1.call-start
  7.2 0.8 constant_dynamic-slice_fusion
  8.0 0.1 copy.39.first
  8.1 0.7 copy.28.first_t
  8.8 0.7 copy.29
  9.6 0.1 fusion.4
  9.7 1.4 copy.30
  11.1 1.8 fusion.1.kernel
  12.9 0.9 dynamic-slice_bitcast_fusion
  13.8 0.0 copy-start.6
  13.8 1.0 copy-done.6
  14.8 0.7 copy-done.13
  15.5 13.7 %spec_grad.1.spectrum = bf16[128,64,256]{2,1,0:T(8,128)(2,1)S(1)} custom-call(bf16[1024,256]{1,0:T(8,128)(2,1)S(1)} %copy-done.6, bf16[256,128]{1,0:T(8,128)(2,1)S(1)} %get-tuple-element.32.cs, f32[1,256]{1,0:T(1,128)S(1)} %copy-done.13, bf16[64,128,1024]{2,1,0:T(8,128)(2,1)} %field.3), custom_call_target="tpu_custom_call" | custom-call | tf_op jit(solution)/shard_map/spec_grad/pallas_call | solution.py:310
  29.2 0.0 copy-start.2
  29.2 2.0 copy-done.2
  31.2 14.4 %lead.1 = (bf16[64,128,256]{2,1,0:T(8,128)(2,1)}, f32[16,128,256]{2,1,0:T(8,128)S(1)}) custom-call(bf16[16,64]{1,0:T(8,128)(2,1)S(1)} %copy-done.12, bf16[1024,256]{1,0:T(8,128)(2,1)S(1)} %copy-done.6, bf16[256,128]{1,0:T(8,128)(2,1)S(1)} %get-tuple-element.32.cs, bf16[64,128,1024]{2,1,0:T(8,128)(2,1)} %field.2), custom_call_target="tpu_custom_call" | custom-call | tf_op jit(solution)/shard_map/lead/pallas_call | solution.py:284
  45.6 1.3 copy-done.7
  46.9 15.1 %lead_grad.1 = f32[16,128,256]{2,1,0:T(8,128)S(1)} custom-call(bf16[256,64]{1,0:T(8,128)(2,1)S(1)} %bitcast.39, f32[128,16,256]{2,1,0:T(8,128)S(1)} %fusion.1.kernel, bf16[128,64,256]{2,1,0:T(8,128)(2,1)} %copy-done.2), custom_call_target="tpu_custom_call" | custom-call | tf_op jit(solution)/shard_map/lead_grad/pallas_call | solution.py:326
  62.0 1.4 copy-done.3
  63.4 0.0 all-reduce.6.cloned.1.call-update
  63.4 0.2 all-reduce.4.cloned.1.call-start
  63.6 0.1 dynamic-slice_convert_fusion
  63.7 0.1 copy.32.second_t
  63.8 0.7 copy_bitcast_fusion.column
  64.6 144.2 %all-reduce.6.cloned.1.call-done = (f32[16,128,256]{2,1,0:T(8,128)}, f32[16,128,256]{2,1,0:T(8,128)}) async-done(((f32[16,128,256]{2,1,0:T(8,128)}, f32[16,128,256]{2,1,0:T(8,128)}), (f32[16,128,256]{2,1,0:T(8,128)}, f32[16,128,256]{2,1,0:T(8,128)})) %all-reduce.6.cloned.1.call-update) | async-done | bytes 4194320 | tf_op jit(solution)/shard_map/psum | solution.py:239
  208.8 1.6 copy-done.5
  210.3 7.3 %first.1 = (bf16[16,128,256]{2,1,0:T(8,128)(2,1)S(1)}, f32[16,64]{1,0:T(8,128)S(1)}) custom-call(bf16[256,128]{1,0:T(8,128)(2,1)S(1)} %get-tuple-element.33.cs, f32[16,128,256]{2,1,0:T(8,128)S(1)} %copy-done.5, bf16[64,128,256]{2,1,0:T(8,128)(2,1)} %get-tuple-element.16.modes), custom_call_target="tpu_custom_call" | custom-call | tf_op jit(solution)/shard_map/first/pallas_call | solution.py:376
  217.6 1.0 copy-done.10
  218.6 0.6 broadcast_multiply_fusion.1
  219.2 27.6 %mix.1 = (bf16[64,128,256]{2,1,0:T(8,128)(2,1)}, f32[64,256]{1,0:T(8,128)S(1)}, f32[8,16,256]{2,1,0:T(8,128)S(1)}, f32[16,256]{1,0:T(8,128)S(1)}) custom-call(f32[16,128,256]{2,1,0:T(8,128)S(1)} %copy-done.8, f32[128,16,256]{2,1,0:T(8,128)S(1)} %fusion.1.kernel, bf16[128,64,256]{2,1,0:T(8,128)(2,1)} %copy-done.2, bf16[256,64]{1,0:T(8,128)(2,1)S(1)} %bitcast.38, ...), custom_call_target="tpu_custom_call" | custom-call | tf_op jit(solution)/shard_map/mix/pallas_call | solution.py:342
  246.9 0.8 dynamic_update_slice.6
  247.7 0.8 pad_maximum_fusion
  248.5 0.0 all-reduce.4.cloned.1.call-update
  248.5 0.0 copy-start.4
  248.5 2.2 copy-done.4
  250.7 1.0 copy-done.9
  251.7 17.1 %output.1 = bf16[64,128,1024]{2,1,0:T(8,128)(2,1)} custom-call(bf16[256,128]{1,0:T(8,128)(2,1)S(1)} %get-tuple-element.33.cs, bf16[256,1024]{1,0:T(8,128)(2,1)S(1)} %copy-done.9, bf16[64,128,256]{2,1,0:T(8,128)(2,1)S(1)} %copy-done.4), custom_call_target="tpu_custom_call" | custom-call | tf_op jit(solution)/shard_map/output/pallas_call | solution.py:416
  268.9 0.0 copy-done.11
  268.9 9.8 %input_grad.1 = bf16[64,128,1024]{2,1,0:T(8,128)(2,1)} custom-call(bf16[64,16]{1,0:T(8,128)(2,1)S(1)} %copy.39.first, bf16[256,1024]{1,0:T(8,128)(2,1)S(1)} %copy-done.9, bf16[16,128,256]{2,1,0:T(8,128)(2,1)S(1)} %copy-done.11), custom_call_target="tpu_custom_call" | custom-call | tf_op jit(solution)/shard_map/input_grad/pallas_call | solution.py:431
  278.7 96.4 %all-reduce.4.cloned.1.call-done = f32[416,256]{1,0:T(8,128)} async-done(((f32[416,256]{1,0:T(8,128)}), f32[416,256]{1,0:T(8,128)}) %all-reduce.4.cloned.1.call-update) | async-done | bytes 426000 | tf_op jit(solution)/shard_map/psum | solution.py:239
  375.1 1.0 broadcast_multiply_fusion
  376.1 0.6 fusion
  376.8 0.6 copy.37
  377.4 0.8 copy.35
  378.2 0.3 reshape.52
  378.6 0.9 copy.36
  379.4 1.0 reshape.53
  (22 shorter events, 0.1 us)
Async XLA Ops:
  7.2 2.4 copy-start
  7.2 201.6 %all-reduce.6.cloned.1.call-start = ((), (), s32[]{:S(2)}) async-start(), calls=%async_computation.1 | async-start | bytes 8388608 | tf_op jit(solution)/shard_map/psum | solution.py:239
  13.8 1.0 copy-start.6
  14.8 0.7 copy-start.13
  15.5 15.7 %copy-start.12 = (bf16[16,64]{1,0:T(8,128)(2,1)S(1)}, bf16[16,64]{1,0:T(8,128)(2,1)}, u32[]{:S(2)}) copy-start(bf16[16,64]{1,0:T(8,128)(2,1)} %copy.28.first_t) | copy-start | bytes 6148
  29.2 2.0 copy-start.2
  45.6 1.3 copy-start.7
  62.0 1.4 copy-start.3
  63.4 311.7 %all-reduce.4.cloned.1.call-start = ((), (), s32[]{:S(2)}) async-start(), calls=%async_computation | async-start | bytes 851968 | tf_op jit(solution)/shard_map/psum | solution.py:239
  208.8 1.6 copy-start.5
  210.3 8.9 %copy-start.8 = (f32[16,128,256]{2,1,0:T(8,128)S(1)}, f32[16,128,256]{2,1,0:T(8,128)}, u32[]{:S(2)}) copy-start(f32[16,128,256]{2,1,0:T(8,128)} %get-tuple-element.28.lead) | copy-start | bytes 6291460
  217.6 1.0 copy-start.10
  248.5 2.2 copy-start.4
  250.7 1.0 copy-start.9
  251.7 17.1 %copy-start.11 = (bf16[16,128,256]{2,1,0:T(8,128)(2,1)S(1)}, bf16[16,128,256]{2,1,0:T(8,128)(2,1)}, u32[]{:S(2)}) copy-start(bf16[16,128,256]{2,1,0:T(8,128)(2,1)} %copy-done.10) | copy-start | bytes 3145732
  268.9 111.6 %copy-start.1 = (f32[16,256,16]{1,2,0:T(8,128)S(1)}, f32[16,256,16]{1,2,0:T(8,128)}, u32[]{:S(2)}) copy-start(f32[16,256,16]{1,2,0:T(8,128)} %param.14) | copy-start | bytes 786436
Sparse Core Ops, SparseCore 0:
  63.5 145.1 all-reduce.5
  248.6 126.4 all-reduce.3

commit v2 on v1

--- a/solution.py
+++ b/solution.py
@@ -235,8 +235,101 @@
     return pl.BlockSpec(shape, lambda i: (0,) * len(shape))
 
 
-def sum_all(x):
-    return lax.psum(x, ("grid", "chan"))
+def halvings(order, units):
+    start, size, plan = 0, units, []
+    for axis, bit in order:
+        size //= 2
+        side = lax.axis_index(axis) // bit % 2
+        plan.append((axis, bit, side, start + side * size, start + (1 - side) * size, size))
+        start = start + side * size
+    return plan
+
+
+def partner(axis, bit, side):
+    return {axis: lax.axis_index(axis) + bit * (1 - 2 * side)}
+
+
+def reduce_kernel(orders, *refs):
+    count = len(orders)
+    inputs, outputs = refs[:count], refs[count : 2 * count]
+    totals, landed = refs[2 * count : 3 * count], refs[3 * count : 4 * count]
+    send_sem, recv_sem = refs[4 * count :]
+    plans = [halvings(order, ref.shape[0]) for order, ref in zip(orders, inputs)]
+    steps = len(orders[0])
+    barrier = pltpu.get_barrier_semaphore()
+    for axis, bit, side, *_ in plans[0]:
+        pl.semaphore_signal(
+            barrier, inc=1, device_id=partner(axis, bit, side),
+            device_id_type=pl.DeviceIdType.MESH,
+        )
+    pl.semaphore_wait(barrier, steps)
+
+    for step in range(steps):
+        copies = []
+        for c in range(count):
+            axis, bit, side, _, other, size = plans[c][step]
+            source = inputs[c] if step == 0 else totals[c]
+            first = inputs[c].shape[0] - 2 * size
+            copy = pltpu.make_async_remote_copy(
+                src_ref=source.at[pl.ds(other, size)],
+                dst_ref=landed[c].at[pl.ds(first, size)],
+                send_sem=send_sem.at[0, c, step],
+                recv_sem=recv_sem.at[0, c, step],
+                device_id=partner(axis, bit, side),
+                device_id_type=pl.DeviceIdType.MESH,
+            )
+            copy.start()
+            copies.append(copy)
+        for c in range(count):
+            _, _, _, own, _, size = plans[c][step]
+            source = inputs[c] if step == 0 else totals[c]
+            target = outputs[c] if step == steps - 1 else totals[c]
+            first = inputs[c].shape[0] - 2 * size
+            copies[c].wait()
+            target[pl.ds(own, size)] = source[pl.ds(own, size)] + landed[c][pl.ds(first, size)]
+
+    for step in reversed(range(steps)):
+        copies = []
+        for c in range(count):
+            axis, bit, side, own, _, size = plans[c][step]
+            copy = pltpu.make_async_remote_copy(
+                src_ref=outputs[c].at[pl.ds(own, size)],
+                dst_ref=outputs[c].at[pl.ds(own, size)],
+                send_sem=send_sem.at[1, c, step],
+                recv_sem=recv_sem.at[1, c, step],
+                device_id=partner(axis, bit, side),
+                device_id_type=pl.DeviceIdType.MESH,
+            )
+            copy.start()
+            copies.append(copy)
+        for copy in copies:
+            copy.wait()
+
+
+def bits(axis):
+    return [(axis, 1 << n) for n in range((lax.axis_size(axis) - 1).bit_length())]
+
+
+def sum_all(arrays, collective_id):
+    chan, grid = bits("chan"), bits("grid")
+    orders = [chan + grid, chan[:1] + grid + chan[1:]][: len(arrays)]
+    wide = arrays[0].shape[-1]
+    flat = [a.reshape(-1, 8, wide) for a in arrays]
+    vmem = pl.BlockSpec(memory_space=pltpu.VMEM)
+    results = pl.pallas_call(
+        lambda *refs: reduce_kernel(orders, *refs),
+        in_specs=[vmem] * len(flat),
+        out_specs=[vmem] * len(flat),
+        out_shape=[jax.ShapeDtypeStruct(a.shape, F32) for a in flat],
+        scratch_shapes=[pltpu.VMEM(a.shape, F32) for a in flat]
+        + [pltpu.VMEM(a.shape, F32) for a in flat]
+        + [pltpu.SemaphoreType.DMA((2, len(flat), len(orders[0])))] * 2,
+        compiler_params=pltpu.CompilerParams(
+            collective_id=collective_id, has_side_effects=True, vmem_limit_bytes=48 * 2**20
+        ),
+        name="sum_all",
+    )(*flat)
+    return [r.reshape(a.shape) for r, a in zip(results, arrays)]
 
 
 def local(input_field, out_cotangent, core_first, core_second, core_third, column_mode_core):
@@ -305,7 +398,6 @@
         compiler_params=params(),
         name="lead",
     )(first_bf.T, table, cs, input_field)
-    lead = sum_all(lead)
 
     spec_grad = pl.pallas_call(
         grad_kernel,
@@ -337,7 +429,7 @@
         compiler_params=params(),
         name="lead_grad",
     )(second_ba, kernel, spec_grad)
-    lead_grad = sum_all(lead_grad)
+    lead, lead_grad = sum_all([lead, lead_grad], 0)
 
     spec_out, part_second, part_third, part_fourth = pl.pallas_call(
         mix_kernel,
@@ -401,7 +493,9 @@
     packed = jnp.concatenate(
         [v.reshape(-1, wide) for v in (first_wide, second_wide, part_third, part_fourth)]
     )
-    packed = sum_all(packed) * (1.0 / modes_x)
+    block = 8 * grid_count * lax.axis_size("chan")
+    packed = jnp.pad(packed, ((0, -packed.shape[0] % block), (0, 0)))
+    packed = sum_all([packed], 1)[0] * (1.0 / modes_x)
     cuts = np.cumsum([0] + [s // wide for s in sizes])
     one, two, three, four = (packed[cuts[n] : cuts[n + 1]] for n in range(4))
     grad_first = one.reshape(rank_a, channels).T

time: 388 us -> 239 us (0.62)
  waiting for transfers between devices: 241 us -> 0 us
  Pallas kernels: 105 us -> 214 us
  between operations: 14.2 us -> 0.87 us
    psum x2 -> x0, waiting for transfers between devices: 241 us -> none  [sum_all(): return lax.psum(x, ('grid', 'chan'))]
    pallas_call x0 -> x2, Pallas kernels: none -> 108 us  [sum_all(): pl.pallas_call(lambda *refs: reduce_kernel(orders, *refs), in_specs=[vmem...]
    unnamed x30 -> x20, local copies, waits for them, and re-layouts: 13 us -> 8.86 us
  transfers between devices with their start and end apart: 2 -> 0, of which waited for: 2 -> 0; matrix products, arithmetic and copies ran while one was open for 0% -> 0% of each run, Pallas kernels for 7% -> 0%
where the time goes in v2:
time: 239 us
  Pallas kernels  214 us (90%)
  local copies, waits for them, and re-layouts  21.6 us (9%)
    pallas_call x2, Pallas kernels, sum_all(): pl.pallas_call(lambda *refs: reduce_kernel(orders, *refs), in_specs=[vmem...  108 us
    pallas_call x1, Pallas kernels, local(): pl.pallas_call(mix_kernel, grid=(mode_steps,), in_specs=[pl.BlockSpec((ra...  27.8 us
    pallas_call x1, Pallas kernels, local(): pl.pallas_call(field_kernel, grid=(chan // out_step,), in_specs=[whole((2...  17.1 us
    pallas_call x1, Pallas kernels, local(): pl.pallas_call(lead_kernel, grid=(row_steps,), in_specs=[whole((rank_a, c...  15.2 us
    pallas_call x1, Pallas kernels, local(): pl.pallas_call(back_kernel, grid=(mode_steps,), in_specs=[whole((pairs, c...  15.1 us
    pallas_call x1, Pallas kernels, local(): pl.pallas_call(grad_kernel, grid=(chan // chan_step,), in_specs=[whole((s...  13.8 us
    pallas_call x1, Pallas kernels, local(): pl.pallas_call(input_kernel, grid=(row_steps,), in_specs=[whole((chan, ra...  9.82 us
    unnamed x20, local copies, waits for them, and re-layouts  8.86 us

profile of v2, /device:TPU:0, one launch (start us, length us, event | category | flops | bytes accessed | tf_op | source)
XLA Modules:
  0.0 238.5 jit_solution(7829702207497950569)
XLA Ops:
  0.6 0.0 copy-start
  0.6 0.0 copy-start.5
  0.7 0.0 copy-start.8
  0.7 0.8 constant_dynamic-slice_fusion
  1.5 0.1 copy.40.first
  1.6 0.1 copy.29.first_t
  1.7 0.7 copy.31
  2.5 0.7 copy_bitcast_fusion.column
  3.2 0.0 copy-done
  3.2 0.1 dynamic-slice_convert_fusion
  3.3 0.1 copy.35.second_t
  3.4 0.1 fusion.5
  3.5 0.9 dynamic-slice_bitcast_fusion
  4.4 1.4 copy.33
  5.8 1.8 fusion.2.kernel
  7.6 0.0 copy-done.5
  7.6 0.0 copy-done.8
  7.6 13.8 %spec_grad.1.spectrum = bf16[128,64,256]{2,1,0:T(8,128)(2,1)S(1)} custom-call(bf16[1024,256]{1,0:T(8,128)(2,1)S(1)} %copy-done.5, bf16[256,128]{1,0:T(8,128)(2,1)S(1)} %get-tuple-element.34.cs, f32[1,256]{1,0:T(1,128)S(1)} %copy-done.8, bf16[64,128,1024]{2,1,0:T(8,128)(2,1)} %field.3), custom_call_target="tpu_custom_call" | custom-call | tf_op jit(solution)/shard_map/spec_grad/pallas_call | solution.py:402
  21.4 0.0 copy-start.2
  21.4 2.0 copy-done.2
  23.4 15.1 %lead_grad.1 = f32[16,128,256]{2,1,0:T(8,128)S(1)} custom-call(bf16[256,64]{1,0:T(8,128)(2,1)S(1)} %bitcast.51, f32[128,16,256]{2,1,0:T(8,128)S(1)} %fusion.2.kernel, bf16[128,64,256]{2,1,0:T(8,128)(2,1)} %copy-done.2), custom_call_target="tpu_custom_call" | custom-call | tf_op jit(solution)/shard_map/lead_grad/pallas_call | solution.py:418
  38.5 0.0 copy-start.3
  38.5 15.2 %lead.1 = (bf16[64,128,256]{2,1,0:T(8,128)(2,1)}, f32[16,128,256]{2,1,0:T(8,128)S(1)}) custom-call(bf16[16,64]{1,0:T(8,128)(2,1)S(1)} %copy.29.first_t, bf16[1024,256]{1,0:T(8,128)(2,1)S(1)} %copy-done.5, bf16[256,128]{1,0:T(8,128)(2,1)S(1)} %get-tuple-element.34.cs, bf16[64,128,1024]{2,1,0:T(8,128)(2,1)} %field.2), custom_call_target="tpu_custom_call" | custom-call | tf_op jit(solution)/shard_map/lead/pallas_call | solution.py:377
  53.7 0.0 copy-done.3
  53.7 0.0 copy-start.6
  53.7 1.3 copy-done.6
  55.0 75.7 %sum_all.2 = (f32[256,8,256]{2,1,0:T(8,128)S(1)}, f32[256,8,256]{2,1,0:T(8,128)S(1)}) custom-call(f32[256,8,256]{2,1,0:T(8,128)} %bitcast.47, f32[256,8,256]{2,1,0:T(8,128)} %bitcast.45), custom_call_target="tpu_custom_call" | custom-call | tf_op jit(solution)/shard_map/sum_all/pallas_call | solution.py:319
  130.7 27.8 %mix.1 = (bf16[64,128,256]{2,1,0:T(8,128)(2,1)}, f32[64,256]{1,0:T(8,128)S(1)}, f32[8,16,256]{2,1,0:T(8,128)S(1)}, f32[16,256]{1,0:T(8,128)S(1)}) custom-call(f32[16,128,256]{2,1,0:T(8,128)S(1)} %bitcast.48, f32[128,16,256]{2,1,0:T(8,128)S(1)} %fusion.2.kernel, bf16[128,64,256]{2,1,0:T(8,128)(2,1)} %copy-done.2, bf16[256,64]{1,0:T(8,128)(2,1)S(1)} %bitcast.50, ...), custom_call_target="tpu_custom_call" | custom-call | tf_op jit(solution)/shard_map/mix/pallas_call | solution.py:434
  158.6 7.1 %first.1 = (bf16[16,128,256]{2,1,0:T(8,128)(2,1)S(1)}, f32[16,64]{1,0:T(8,128)S(1)}) custom-call(bf16[256,128]{1,0:T(8,128)(2,1)S(1)} %get-tuple-element.35.cs, f32[16,128,256]{2,1,0:T(8,128)S(1)} %bitcast.46, bf16[64,128,256]{2,1,0:T(8,128)(2,1)} %get-tuple-element.20.modes), custom_call_target="tpu_custom_call" | custom-call | tf_op jit(solution)/shard_map/first/pallas_call | solution.py:468
  165.8 0.3 dynamic_update_slice.6
  166.1 32.6 %sum_all.3 = f32[64,8,256]{2,1,0:T(8,128)S(1)} custom-call(f32[64,8,256]{2,1,0:T(8,128)S(1)} %fusion.refs_0_), custom_call_target="tpu_custom_call" | custom-call | tf_op jit(solution)/shard_map/sum_all/pallas_call | solution.py:319
  198.7 0.6 fusion.1
  199.3 0.6 copy.44
  200.0 0.3 reshape.82
  200.3 0.0 copy-start.7
  200.3 1.7 copy.36
  202.1 2.2 reshape.83
  204.2 2.0 reshape.81
  206.2 3.2 %copy.38 = f32[16,256,16]{1,2,0:T(8,128)} copy(f32[16,256,16]{2,0,1:T(8,128)} %bitcast.54) | data formatting | bytes 524288
  209.4 0.0 copy-done.7
  209.4 0.0 copy-start.4
  209.4 2.2 copy-done.4
  211.6 17.1 %output.1 = bf16[64,128,1024]{2,1,0:T(8,128)(2,1)} custom-call(bf16[256,128]{1,0:T(8,128)(2,1)S(1)} %get-tuple-element.35.cs, bf16[256,1024]{1,0:T(8,128)(2,1)S(1)} %copy-done.7, bf16[64,128,256]{2,1,0:T(8,128)(2,1)S(1)} %copy-done.4), custom_call_target="tpu_custom_call" | custom-call | tf_op jit(solution)/shard_map/output/pallas_call | solution.py:510
  228.7 0.0 copy-start.1
  228.7 9.8 %input_grad.1 = bf16[64,128,1024]{2,1,0:T(8,128)(2,1)} custom-call(bf16[64,16]{1,0:T(8,128)(2,1)S(1)} %copy.40.first, bf16[256,1024]{1,0:T(8,128)(2,1)S(1)} %copy-done.7, bf16[16,128,256]{2,1,0:T(8,128)(2,1)S(1)} %get-tuple-element.21.rows), custom_call_target="tpu_custom_call" | custom-call | tf_op jit(solution)/shard_map/input_grad/pallas_call | solution.py:525
  238.5 0.0 copy-done.1
  (11 shorter events, 0.2 us)
Async XLA Ops:
  0.6 2.6 %copy-start = (f32[16,256,16]{1,2,0:T(8,128)S(1)}, f32[16,256,16]{1,2,0:T(8,128)}, u32[]{:S(2)}) copy-start(f32[16,256,16]{1,2,0:T(8,128)} %param.14) | copy-start | bytes 786436
  0.6 6.9 %copy-start.5 = (bf16[1024,256]{1,0:T(8,128)(2,1)S(1)}, bf16[1024,256]{1,0:T(8,128)(2,1)}, u32[]{:S(2)}) copy-start(bf16[1024,256]{1,0:T(8,128)(2,1)} %constant.40.clone.table) | copy-start | bytes 1572868
  0.7 6.9 %copy-start.8 = (f32[1,256]{1,0:T(1,128)S(1)}, f32[1,256]{1,0:T(1,128)}, u32[]{:S(2)}) copy-start(f32[1,256]{1,0:T(1,128)} %constant.44.clone.weight) | copy-start | bytes 3076
  21.4 2.0 copy-start.2
  38.5 15.2 %copy-start.3 = (f32[16,128,256]{2,1,0:T(8,128)}, f32[16,128,256]{2,1,0:T(8,128)S(1)}, u32[]{:S(2)}) copy-start(f32[16,128,256]{2,1,0:T(8,128)S(1)} %lead_grad.1) | copy-start | bytes 6291460
  53.7 1.3 copy-start.6
  200.3 9.1 %copy-start.7 = (bf16[256,1024]{1,0:T(8,128)(2,1)S(1)}, bf16[256,1024]{1,0:T(8,128)(2,1)}, u32[]{:S(2)}) copy-start(bf16[256,1024]{1,0:T(8,128)(2,1)} %constant.41.clone.table) | copy-start | bytes 1572868
  209.4 2.2 copy-start.4
  228.7 9.8 %copy-start.1 = (f32[16,256,16]{1,2,0:T(8,128)S(1)}, f32[16,256,16]{1,2,0:T(8,128)}, u32[]{:S(2)}) copy-start(f32[16,256,16]{1,2,0:T(8,128)} %param.14) | copy-start | bytes 786436
